TPU v7x, 512 devices: a whole 4x4x16 slice. The times are simulated.
512 devices in a mesh: row: 16 (over z), col: 4 (over x_hi, core), layer: 8 (over x_lo, y).
Axes of the slice: x: 4 (x_hi: 2, x_lo: 2; x = x_hi * 2 + x_lo), y: 4, z: 16, core: 2. Of those that a mesh axis runs over, the one named last changes fastest.
Arguments:
- blocks: float32 [4096, 128, 128], P(('row', 'col', 'layer')), may hold values from -0.6 to 0.6
- block_ids: int32 [4096, 2], P(('row', 'col', 'layer')), may hold values from -1 to 1535, as said below
- out_ids: int32 [4096, 2], P(('row', 'col')), may hold values from -1 to 1535, as said below
Outputs:
- products: float32 [4096, 128, 128], P(('row', 'col', 'layer'))
Inputs may be any that keep to these rules, and one draw needn't show every extreme that they name: `block_ids`: each row is the (block row, block column) of one slot, or (-1, -1) for an empty slot. The device at index (r, c, l) of (row, col, layer) holds blocks whose row is r modulo 16 and whose column is c * 8 + l modulo 4 * 8. Each row group r has between 1 and 4 block rows in use, and each column class has exactly 2 block columns in use; a device holds every block where its row group's rows in use meet its class's columns, each once, in no set order, and its other slots are empty. Some 4 + 1 row groups in a row (wrapping around) have 4 rows in use. `out_ids`: the 64 rows for the index pair (r, c) of (row, col) list, in no set order, each pair (i, j) once where i is a block row in use of row group r and j one of row group (r + 4 c + m) modulo 16 for some m < 4; the remaining rows are (-1, -1).
All inputs are finite; a program needn't handle non-finite values.
Results may differ from a plain program's by a relative error of at most 0.0003.
Values sent between devices are 32-bit elements; how exact they have to be, the bound alone decides.
No kernel may reach another device: no remote copies, remote signals or barrier semaphores. Data moves between devices by JAX's collectives and lax.ppermute only.
A program may use at most 64 MiB of HBM per device.

v0:
```python
import jax
import jax.numpy as jnp
from jax import lax
from jax.sharding import PartitionSpec as P

NB = 1536
ROWS_G = 4
HIGH = lax.Precision.HIGHEST


def shifted(value, axis, steps):
    count = lax.axis_size(axis)
    pairs = [(source, (source + steps) % count) for source in range(count)]
    return lax.ppermute(value, axis, pairs)


def arrange(panel_blocks, panel_coords, row_total):
    slot_total = panel_blocks.shape[0]
    width = panel_blocks.shape[1]
    per_row = slot_total // row_total
    row_ids = panel_coords[:, 0]
    col_ids = panel_coords[:, 1]
    slot_range = jnp.arange(slot_total, dtype=jnp.int32)
    sort_key = jnp.where(row_ids >= 0, row_ids * NB + col_ids, 2**30 + slot_range)
    rank_of = jnp.sum((sort_key[None, :] < sort_key[:, None]).astype(jnp.int32), axis=1)
    gather_order = jnp.sum(
        jnp.where(rank_of[None, :] == slot_range[:, None], slot_range[None, :], 0), axis=1
    )
    ordered = jnp.take(panel_blocks, gather_order, axis=0)
    row_heads = jnp.take(row_ids, gather_order)[::per_row]
    shaped = ordered.reshape(row_total, per_row, width, width).transpose(0, 2, 1, 3)
    shaped = shaped.reshape(row_total, width, per_row * width)
    shaped = jnp.where((row_heads >= 0)[:, None, None], shaped, jnp.float32(0.0))
    return (shaped.reshape(row_total * width, per_row * width), row_heads)


def locate(targets, heads):
    hits = (targets[:, None] == heads[None, :]) & (targets[:, None] >= 0)
    found = jnp.any(hits, axis=1)
    head_range = jnp.arange(heads.shape[0], dtype=jnp.int32)
    where_at = jnp.sum(jnp.where(hits, head_range[None, :], 0), axis=1)
    return (where_at, found)


def shards(blocks, block_ids, out_ids):
    row_count = lax.axis_size("row")
    col_count = lax.axis_size("col")
    stride = row_count // col_count
    col_index = lax.axis_index("col")
    width = blocks.shape[1]
    left_blocks, left_coords = (
        lax.all_gather(blocks, "col", axis=0, tiled=True),
        lax.all_gather(block_ids, "col", axis=0, tiled=True),
    )
    base_blocks, base_coords = (left_blocks, left_coords)
    far_blocks, far_coords = (left_blocks, left_coords)
    for offset in range(1, col_count):
        far_blocks, far_coords = shifted((far_blocks, far_coords), "row", row_count - stride)
        chosen = col_index == offset
        base_blocks = jnp.where(chosen, far_blocks, base_blocks)
        base_coords = jnp.where(chosen, far_coords, base_coords)
    block_list = [base_blocks]
    coord_list = [base_coords]
    for offset in range(1, stride):
        far_blocks, far_coords = shifted((block_list[-1], coord_list[-1]), "row", row_count - 1)
        block_list.append(far_blocks)
        coord_list.append(far_coords)
    stack_blocks = jnp.stack(block_list, axis=0)
    stack_coords = jnp.stack(coord_list, axis=0)
    left_dense, left_heads = arrange(left_blocks, left_coords, ROWS_G)
    right_dense, right_heads = jax.vmap(
        lambda stack_piece, coord_piece: arrange(stack_piece, coord_piece, ROWS_G)
    )(stack_blocks, stack_coords)
    right_dense = right_dense.reshape(-1, right_dense.shape[-1])
    right_heads = right_heads.reshape(-1)
    right_total = right_heads.shape[0]
    partial_all = lax.dot_general(
        left_dense,
        right_dense,
        (((1,), (1,)), ((), ())),
        precision=HIGH,
        preferred_element_type=jnp.float32,
    )
    tiled = (
        partial_all.reshape(ROWS_G, width, right_total, width)
        .transpose(0, 2, 1, 3)
        .reshape(ROWS_G * right_total, width, width)
    )
    left_at, left_found = locate(out_ids[:, 0], left_heads)
    right_at, right_found = locate(out_ids[:, 1], right_heads)
    picked = jnp.take(tiled, left_at * right_total + right_at, axis=0)
    picked = jnp.where((left_found & right_found)[:, None, None], picked, jnp.float32(0.0))
    return lax.psum_scatter(picked, "layer", scatter_dimension=0, tiled=True)


def solution(mesh):
    return jax.shard_map(
        shards,
        mesh=mesh,
        in_specs=(
            P(("row", "col", "layer"), None, None),
            P(("row", "col", "layer"), None),
            P(("row", "col"), None),
        ),
        out_specs=P(("row", "col", "layer"), None, None),
        check_vma=False,
    )
```

profile of v0, /device:TPU:1, one launch (start us, length us, event | category | flops | bytes accessed | tf_op | source)
XLA Modules:
  0.0 921.1 jit_solution(10634318678526448864)
XLA Ops:
  6.5 0.7 all-gather.3.cloned.1.call-update
  7.3 42.2 %all-gather.3.cloned.1.call-done = f32[32,128,128]{2,1,0:T(8,128)} async-done(((f32[8,128,128]{2,1,0:T(8,128)}), f32[32,128,128]{2,1,0:T(8,128)}) %all-gather.3.cloned.1.call-update) | async-done | bytes 2097168 | tf_op jit(solution)/shard_map/all_gather | solution.py:52
  49.5 8.1 collective-permute-start.6
  57.6 283.4 %collective-permute-done.6 = f32[32,128,128]{2,1,0:T(8,128)S(1)} collective-permute-done((f32[32,128,128]{2,1,0:T(8,128)}, f32[32,128,128]{2,1,0:T(8,128)S(1)}, u32[]{:S(2)}, u32[]{:S(2)}) %collective-permute-start.6) | collective-permute-done | bytes 2097184 | tf_op jit(solution)/shard_map/ppermute | solution.py:14
  341.0 1.3 copy-done.1
  342.3 9.6 %collective-permute-start.7 = (f32[32,128,128]{2,1,0:T(8,128)S(1)}, f32[32,128,128]{2,1,0:T(8,128)S(1)}, u32[]{:S(2)}, u32[]{:S(2)}) collective-permute-start(f32[32,128,128]{2,1,0:T(8,128)S(1)} %collective-permute-done.6), channel_id=1, source_target_pairs={{0,384},{32,416},{64,448},{96,480},{128,0},{160,32},{192,64},{224,... | collective-permute-start | bytes 6291464 | tf_op jit(solution)/shard_map/ppermute | solution.py:14
  351.9 178.9 %collective-permute-done.7 = f32[32,128,128]{2,1,0:T(8,128)S(1)} collective-permute-done((f32[32,128,128]{2,1,0:T(8,128)S(1)}, f32[32,128,128]{2,1,0:T(8,128)S(1)}, u32[]{:S(2)}, u32[]{:S(2)}) %collective-permute-start.7) | collective-permute-done | bytes 2097184 | tf_op jit(solution)/shard_map/ppermute | solution.py:14
  530.8 1.9 collective-permute-start.8
  532.8 68.6 %collective-permute-done.8 = f32[32,128,128]{2,1,0:T(8,128)} collective-permute-done((f32[32,128,128]{2,1,0:T(8,128)S(1)}, f32[32,128,128]{2,1,0:T(8,128)}, u32[]{:S(2)}, u32[]{:S(2)}) %collective-permute-start.8) | collective-permute-done | bytes 2097184 | tf_op jit(solution)/shard_map/ppermute | solution.py:14
  601.4 2.4 select_select_fusion.1
  603.8 1.9 collective-permute-start.9
  605.7 12.6 %all-gather = s32[4,8,2]{1,2,0:T(2,128)S(1)} all-gather(s32[1,8,2]{1,2,0:T(2,128)S(1)} %bitcast.72), channel_id=1, replica_groups=mesh['row'=16,'col'=4,'layer'=8] {'col'}, dimensions={0}, use_global_device_ids=true | all-gather | bytes 320 | tf_op jit(solution)/shard_map/all_gather | solution.py:53
  618.4 6.9 collective-permute-start
  625.3 0.2 convert_reduce_fusion.1
  625.5 0.1 select_reduce_fusion.1
  625.7 21.0 %collective-permute-done.9 = f32[32,128,128]{2,1,0:T(8,128)} collective-permute-done((f32[32,128,128]{2,1,0:T(8,128)S(1)}, f32[32,128,128]{2,1,0:T(8,128)}, u32[]{:S(2)}, u32[]{:S(2)}) %collective-permute-start.9) | collective-permute-done | bytes 2097184 | tf_op jit(solution)/shard_map/ppermute | solution.py:14
  646.7 8.3 collective-permute-start.10
  655.0 0.7 gather_fusion
  655.7 5.2 collective-permute-done
  661.0 1.9 collective-permute-start.1
  663.0 47.3 %collective-permute-done.1 = s32[32,2]{0,1:T(2,128)S(1)} collective-permute-done((s32[32,2]{0,1:T(2,128)S(1)}, s32[32,2]{0,1:T(2,128)S(1)}, u32[]{:S(2)}, u32[]{:S(2)}) %collective-permute-start.1) | collective-permute-done | bytes 288 | tf_op jit(solution)/shard_map/ppermute | solution.py:14
  710.2 1.9 collective-permute-start.2
  712.2 6.3 collective-permute-done.2
  718.5 2.2 collective-permute-start.3
  720.7 2.0 collective-permute-done.3
  722.8 3.4 collective-permute-start.4
  726.2 0.9 collective-permute-done.4
  727.2 4.5 collective-permute-start.5
  731.7 0.7 collective-permute-done.5
  732.4 5.0 collective-permute-start.11
  737.4 0.2 convert_reduce_fusion
  737.6 0.2 select_reduce_fusion
  738.0 1.5 gather_fusion.3
  739.6 0.1 slice.31
  740.1 2.3 gather_fusion.1
  742.4 0.3 select_bitcast_fusion.1
  742.7 2.6 copy.26
  745.2 1.7 reshape.226
  747.0 28.7 %collective-permute-done.11 = f32[32,128,128]{2,1,0:T(8,128)} collective-permute-done((f32[32,128,128]{2,1,0:T(8,128)}, f32[32,128,128]{2,1,0:T(8,128)}, u32[]{:S(2)}, u32[]{:S(2)}) %collective-permute-start.11) | collective-permute-done | bytes 2097184 | tf_op jit(solution)/shard_map/ppermute | solution.py:14
  775.7 5.9 pad_maximum_fusion
  781.6 7.7 gather_fusion.4
  789.2 4.2 select_bitcast_fusion
  793.5 9.7 %copy.27 = f32[4,4,128,8,128]{4,3,2,1,0:T(8,128)} copy(f32[4,4,128,8,128]{4,2,3,1,0:T(8,128)S(1)} %select_bitcast_fusion) | data formatting | bytes 16777216 | tf_op jit(solution)/shard_map/vmap(jit(_where))/select_n | solution.py:33
  803.2 9.3 %reshape.227 = f32[16,128,1024,1]{2,1,0,3:T(8,128)} reshape(f32[4,4,128,8,128]{4,3,2,1,0:T(8,128)} %copy.27) | data formatting | bytes 16777216 | tf_op jit(solution)/shard_map/vmap(jit(_where))/select_n | solution.py:33
  812.5 17.6 %fusion = f32[4,128,16,128]{3,1,2,0:T(8,128)} fusion(f32[16,128,1024,1]{2,1,0,3:T(8,128)} %reshape.227, f32[4,128,1024,1]{2,1,0,3:T(8,128)S(1)} %reshape.226), kind=kOutput, calls=%fused_computation.8 | convolution fusion | flops 12884901888 | bytes 14680064 | tf_op jit(solution)/shard_map/dot_general | solution.py:77
  830.1 4.9 gather_fusion.2
  835.0 4.6 select_select_fusion
  839.7 74.6 %reduce-scatter.2.cloned.1.call-done = f32[8,128,128]{2,1,0:T(8,128)} async-done(((f32[64,128,128]{2,1,0:T(8,128)}), f32[8,128,128]{2,1,0:T(8,128)}) %reduce-scatter.2.cloned.1.call-update) | async-done | bytes 524304 | tf_op jit(solution)/shard_map/reduce_scatter | solution.py:93
  (47 shorter events, 1.2 us)
Async XLA Ops:
  6.5 43.0 %all-gather.3.cloned.1.call-start = ((), (), s32[]{:S(2)}) async-start(), calls=%async_computation.1 | async-start | bytes 2621440 | tf_op jit(solution)/shard_map/all_gather | solution.py:52
  7.3 907.0 %reduce-scatter.2.cloned.1.call-start = ((), (), s32[]{:S(2)}) async-start(), calls=%async_computation.2 | async-start | bytes 4718592 | tf_op jit(solution)/shard_map/reduce_scatter | solution.py:93
  49.5 291.5 %collective-permute-start.6 = (f32[32,128,128]{2,1,0:T(8,128)}, f32[32,128,128]{2,1,0:T(8,128)S(1)}, u32[]{:S(2)}, u32[]{:S(2)}) collective-permute-start(f32[32,128,128]{2,1,0:T(8,128)} %all-gather.3.cloned.1.call-done), channel_id=1, source_target_pairs={{0,384},{32,416},{64,448},{96,480},{128,0},{160,32},{192,64},{224,... | collective-permute-start | bytes 6291464 | tf_op jit(solution)/shard_map/ppermute | solution.py:14
  341.0 1.3 copy-start.1
  342.3 188.5 %collective-permute-start.7 = (f32[32,128,128]{2,1,0:T(8,128)S(1)}, f32[32,128,128]{2,1,0:T(8,128)S(1)}, u32[]{:S(2)}, u32[]{:S(2)}) collective-permute-start(f32[32,128,128]{2,1,0:T(8,128)S(1)} %collective-permute-done.6), channel_id=1, source_target_pairs={{0,384},{32,416},{64,448},{96,480},{128,0},{160,32},{192,64},{224,... | collective-permute-start | bytes 6291464 | tf_op jit(solution)/shard_map/ppermute | solution.py:14
  530.8 1.9 copy-start.2
  530.8 70.6 %collective-permute-start.8 = (f32[32,128,128]{2,1,0:T(8,128)S(1)}, f32[32,128,128]{2,1,0:T(8,128)}, u32[]{:S(2)}, u32[]{:S(2)}) collective-permute-start(f32[32,128,128]{2,1,0:T(8,128)S(1)} %collective-permute-done.7), channel_id=1, source_target_pairs={{0,384},{32,416},{64,448},{96,480},{128,0},{160,32},{192,64},{224,... | collective-permute-start | bytes 6291464 | tf_op jit(solution)/shard_map/ppermute | solution.py:14
  532.8 73.0 %copy-start.4 = (s32[8,2]{0,1:T(2,128)S(1)}, s32[8,2]{0,1:T(2,128)}, u32[]{:S(2)}) copy-start(s32[8,2]{0,1:T(2,128)} %param.4) | copy-start | bytes 196
  532.8 92.9 %copy-start.3 = (s32[64,2]{0,1:T(2,128)S(1)}, s32[64,2]{0,1:T(2,128)}, u32[]{:S(2)}) copy-start(s32[64,2]{0,1:T(2,128)} %param.5) | copy-start | bytes 1540
  603.8 128.6 %copy-start = (f32[32,128,128]{2,1,0:T(8,128)}, f32[32,128,128]{2,1,0:T(8,128)S(1)}, u32[]{:S(2)}) copy-start(f32[32,128,128]{2,1,0:T(8,128)S(1)} %select_select_fusion.1) | copy-start | bytes 6291460
  603.8 42.9 %collective-permute-start.9 = (f32[32,128,128]{2,1,0:T(8,128)S(1)}, f32[32,128,128]{2,1,0:T(8,128)}, u32[]{:S(2)}, u32[]{:S(2)}) collective-permute-start(f32[32,128,128]{2,1,0:T(8,128)S(1)} %select_select_fusion.1), channel_id=1, source_target_pairs={{0,480},{32,0},{64,32},{96,64},{128,96},{160,128},{192,160},{224,1... | collective-permute-start | bytes 6291464 | tf_op jit(solution)/shard_map/ppermute | solution.py:14
  618.4 42.6 %collective-permute-start = (s32[32,2]{0,1:T(2,128)S(1)}, s32[32,2]{0,1:T(2,128)S(1)}, u32[]{:S(2)}, u32[]{:S(2)}) collective-permute-start(s32[32,2]{0,1:T(2,128)S(1)} %reshape.225), channel_id=1, source_target_pairs={{0,384},{32,416},{64,448},{96,480},{128,0},{160,32},{192,64},{224,... | collective-permute-start | bytes 776 | tf_op jit(solution)/shard_map/ppermute | solution.py:14
  646.7 85.7 %collective-permute-start.10 = (f32[32,128,128]{2,1,0:T(8,128)}, f32[32,128,128]{2,1,0:T(8,128)}, u32[]{:S(2)}, u32[]{:S(2)}) collective-permute-start(f32[32,128,128]{2,1,0:T(8,128)} %collective-permute-done.9), channel_id=1, source_target_pairs={{0,480},{32,0},{64,32},{96,64},{128,96},{160,128},{192,160},{224,1... | collective-permute-start | bytes 6291464 | tf_op jit(solution)/shard_map/ppermute | solution.py:14
  661.0 49.3 %collective-permute-start.1 = (s32[32,2]{0,1:T(2,128)S(1)}, s32[32,2]{0,1:T(2,128)S(1)}, u32[]{:S(2)}, u32[]{:S(2)}) collective-permute-start(s32[32,2]{0,1:T(2,128)S(1)} %collective-permute-done), channel_id=1, source_target_pairs={{0,384},{32,416},{64,448},{96,480},{128,0},{160,32},{192,64},{224,... | collective-permute-start | bytes 776 | tf_op jit(solution)/shard_map/ppermute | solution.py:14
  710.2 8.2 collective-permute-start.2
  718.5 4.3 collective-permute-start.3
  722.8 4.4 collective-permute-start.4
  727.2 5.2 collective-permute-start.5
  732.4 43.3 %collective-permute-start.11 = (f32[32,128,128]{2,1,0:T(8,128)}, f32[32,128,128]{2,1,0:T(8,128)}, u32[]{:S(2)}, u32[]{:S(2)}) collective-permute-start(f32[32,128,128]{2,1,0:T(8,128)} %collective-permute-done.10), channel_id=1, source_target_pairs={{0,480},{32,0},{64,32},{96,64},{128,96},{160,128},{192,160},{224,1... | collective-permute-start | bytes 6291464 | tf_op jit(solution)/shard_map/ppermute | solution.py:14
Sparse Core Ops, SparseCore 0:
  9.5 39.9 all-gather.2
  839.8 74.4 reduce-scatter.1
where the time goes:
time: 922 us; the launch traced here: 921 us
  waiting for transfers between devices  760 us (82%)
  starting transfers between devices  55.6 us (6%)
  local copies, waits for them, and re-layouts  42.5 us (5%)
  other arithmetic  18.6 us (2%)
  matrix products  17.6 us (2%)
  between operations  13.7 us (1%)
  blocking collectives  12.6 us (1%)
    ppermute x12, waiting for transfers between devices, shifted(): return lax.ppermute(value, axis, pairs)  643 us
    reduce_scatter x1, waiting for transfers between devices, shards(): return lax.psum_scatter(picked, 'layer', scatter_dimension=0, tiled=True)  74.6 us
    ppermute x12, starting transfers between devices, shifted(): return lax.ppermute(value, axis, pairs)  55.6 us
    all_gather x1, waiting for transfers between devices, shards(): lax.all_gather(blocks, 'col', axis=0, tiled=True)  42.2 us
    select_n x4, local copies, waits for them, and re-layouts, arrange(): jnp.where((row_heads >= 0)[:, None, None], shaped, jnp.float32(0.0))  23.3 us
  transfers between devices with their start and end apart: 14, of which 13 were waited for; matrix products, arithmetic and copies ran while one was open for 1% of the time, Pallas kernels for 0%

commit v1 on v0

--- a/solution.py
+++ b/solution.py
@@ -6,6 +6,13 @@
 NB = 1536
 ROWS_G = 4
 HIGH = lax.Precision.HIGHEST
+
+
+def swapped_in(block, mesh_axis, along):
+    count = lax.axis_size(mesh_axis)
+    tiles = jnp.stack([block for _ in range(count)])
+    tiles = lax.all_to_all(tiles, mesh_axis, split_axis=0, concat_axis=0)
+    return jnp.concatenate(tiles, axis=along)
 
 
 def shifted(value, axis, steps):
@@ -49,7 +56,7 @@
     col_index = lax.axis_index("col")
     width = blocks.shape[1]
     left_blocks, left_coords = (
-        lax.all_gather(blocks, "col", axis=0, tiled=True),
+        swapped_in(blocks, "col", 0),
         lax.all_gather(block_ids, "col", axis=0, tiled=True),
     )
     base_blocks, base_coords = (left_blocks, left_coords)

time: 922 us -> 905 us (0.982)
  waiting for transfers between devices: 760 us -> 614 us
  starting transfers between devices: 55.6 us -> 160 us
  blocking collectives: 12.6 us -> 41.3 us
  local copies, waits for them, and re-layouts: 42.5 us -> 30.9 us
    ppermute x12, starting transfers between devices: 55.6 us -> 160 us  [shifted(): return lax.ppermute(value, axis, pairs)]
    ppermute x12, waiting for transfers between devices: 643 us -> 548 us  [shifted(): return lax.ppermute(value, axis, pairs)]
    all_gather x1 -> x0, waiting for transfers between devices: 42.2 us -> none  [shards(): lax.all_gather(blocks, 'col', axis=0, tiled=True)]
    all_to_all x0 -> x1, blocking collectives: none -> 35.5 us  [swapped_in(): tiles = lax.all_to_all(tiles, mesh_axis, split_axis=0, concat_axis=0)]
    select_n x4 -> x2, local copies, waits for them, and re-layouts: 23.3 us -> 10.6 us  [arrange(): jnp.where((row_heads >= 0)[:, None, None], shaped, jnp.float32(0.0))]
  transfers between devices with their start and end apart: 14 -> 13, of which waited for: 13 -> 11; matrix products, arithmetic and copies ran while one was open for 1% -> 1% of each run, Pallas kernels for 0% -> 0%
where the time goes in v1:
time: 905 us; the launch traced here: 904 us
  waiting for transfers between devices  614 us (68%)
  starting transfers between devices  160 us (18%)
  blocking collectives  41.3 us (5%)
  local copies, waits for them, and re-layouts  30.9 us (3%)
  other arithmetic  26.2 us (3%)
  matrix products  17.8 us (2%)
  between operations  13.7 us (2%)
    ppermute x12, waiting for transfers between devices, shifted(): return lax.ppermute(value, axis, pairs)  548 us
    ppermute x12, starting transfers between devices, shifted(): return lax.ppermute(value, axis, pairs)  160 us
    reduce_scatter x1, waiting for transfers between devices, shards(): return lax.psum_scatter(picked, 'layer', scatter_dimension=0, tiled=True)  66.2 us
    all_to_all x1, blocking collectives, swapped_in(): tiles = lax.all_to_all(tiles, mesh_axis, split_axis=0, concat_axis=0)  35.5 us
  transfers between devices with their start and end apart: 13, of which 11 were waited for; matrix products, arithmetic and copies ran while one was open for 1% of the time, Pallas kernels for 0%

profile of v1, /device:TPU:1, one launch (start us, length us, event | category | flops | bytes accessed | tf_op | source)
XLA Modules:
  0.0 904.1 jit_solution(1556267834291571045)
XLA Ops:
  6.5 1.3 stack.42
  7.8 35.5 %all_to_all.5 = f32[4,8,128,128]{3,2,1,0:T(8,128)S(1)} all-to-all(f32[4,8,128,128]{3,2,1,0:T(8,128)S(1)} %stack.42), channel_id=1, replica_groups=mesh['row'=16,'col'=4,'layer'=8] {'col'}, dimensions={0} | all-to-all | bytes 4194304 | tf_op jit(solution)/shard_map/all_to_all | solution.py:14
  43.3 8.7 collective-permute-start.6
  52.0 193.6 %collective-permute-done.6 = f32[32,128,128]{2,1,0:T(8,128)S(1)} collective-permute-done((f32[32,128,128]{2,1,0:T(8,128)S(1)}, f32[32,128,128]{2,1,0:T(8,128)S(1)}, u32[]{:S(2)}, u32[]{:S(2)}) %collective-permute-start.6) | collective-permute-done | bytes 2097184 | tf_op jit(solution)/shard_map/ppermute | solution.py:21
  245.6 1.3 copy-done
  247.0 6.0 collective-permute-start.7
  253.0 74.3 %collective-permute-done.7 = f32[32,128,128]{2,1,0:T(8,128)} collective-permute-done((f32[32,128,128]{2,1,0:T(8,128)S(1)}, f32[32,128,128]{2,1,0:T(8,128)}, u32[]{:S(2)}, u32[]{:S(2)}) %collective-permute-start.7) | collective-permute-done | bytes 2097184 | tf_op jit(solution)/shard_map/ppermute | solution.py:21
  327.3 6.8 collective-permute-start.8
  334.1 171.8 %collective-permute-done.8 = f32[32,128,128]{2,1,0:T(8,128)} collective-permute-done((f32[32,128,128]{2,1,0:T(8,128)}, f32[32,128,128]{2,1,0:T(8,128)}, u32[]{:S(2)}, u32[]{:S(2)}) %collective-permute-start.8) | collective-permute-done | bytes 2097184 | tf_op jit(solution)/shard_map/ppermute | solution.py:21
  505.9 3.8 select_select_fusion.1
  509.7 101.8 %collective-permute-start.9 = (f32[32,128,128]{2,1,0:T(8,128)}, f32[32,128,128]{2,1,0:T(8,128)}, u32[]{:S(2)}, u32[]{:S(2)}) collective-permute-start(f32[32,128,128]{2,1,0:T(8,128)} %select_select_fusion.1), channel_id=1, source_target_pairs={{0,480},{32,0},{64,32},{96,64},{128,96},{160,128},{192,160},{224,1... | collective-permute-start | bytes 6291464 | tf_op jit(solution)/shard_map/ppermute | solution.py:21
  611.6 5.8 all-gather
  617.5 7.1 collective-permute-start
  624.6 0.2 convert_reduce_fusion.1
  624.8 0.1 select_reduce_fusion.1
  625.0 32.0 %collective-permute-done.9 = f32[32,128,128]{2,1,0:T(8,128)} collective-permute-done((f32[32,128,128]{2,1,0:T(8,128)}, f32[32,128,128]{2,1,0:T(8,128)}, u32[]{:S(2)}, u32[]{:S(2)}) %collective-permute-start.9) | collective-permute-done | bytes 2097184 | tf_op jit(solution)/shard_map/ppermute | solution.py:21
  657.0 5.0 collective-permute-start.10
  662.1 0.7 gather_fusion
  662.8 1.9 collective-permute-start.1
  664.7 0.1 slice.27
  664.8 42.2 %collective-permute-done.1 = s32[32,2]{0,1:T(2,128)S(1)} collective-permute-done((s32[32,2]{0,1:T(2,128)S(1)}, s32[32,2]{0,1:T(2,128)S(1)}, u32[]{:S(2)}, u32[]{:S(2)}) %collective-permute-start.1) | collective-permute-done | bytes 288 | tf_op jit(solution)/shard_map/ppermute | solution.py:21
  707.0 7.6 collective-permute-start.2
  714.7 0.7 collective-permute-done.2
  715.4 2.2 collective-permute-start.3
  717.6 2.0 collective-permute-done.3
  719.7 3.4 collective-permute-start.4
  723.2 0.8 collective-permute-done.4
  724.0 4.6 collective-permute-start.5
  728.6 0.7 collective-permute-done.5
  729.3 5.0 collective-permute-start.11
  734.3 0.2 convert_reduce_fusion
  734.5 0.2 select_reduce_fusion
  734.9 1.5 gather_fusion.3
  736.5 0.1 slice.31
  736.7 0.1 fusion
  736.8 0.1 select_reduce_fusion.2
  737.0 2.0 gather_fusion.1
  739.0 3.2 select_bitcast_fusion.1
  742.2 1.9 copy.32
  744.1 29.8 %collective-permute-done.11 = f32[32,128,128]{2,1,0:T(8,128)} collective-permute-done((f32[32,128,128]{2,1,0:T(8,128)}, f32[32,128,128]{2,1,0:T(8,128)}, u32[]{:S(2)}, u32[]{:S(2)}) %collective-permute-start.11) | collective-permute-done | bytes 2097184 | tf_op jit(solution)/shard_map/ppermute | solution.py:21
  773.9 5.9 pad_maximum_fusion
  779.8 7.7 gather_fusion.4
  787.4 7.4 select_bitcast_fusion
  794.9 8.7 copy.33
  803.6 17.8 %fusion.10 = f32[4,128,16,128]{3,1,2,0:T(8,128)} fusion(f32[4,128,1024,1]{1,2,3,0:T(8,128)S(1)} %bitcast.73, f32[16,128,1024,1]{1,2,0,3:T(8,128)} %bitcast.68), kind=kOutput, calls=%fused_computation.61 | convolution fusion | flops 12884901888 | bytes 14680064 | tf_op jit(solution)/shard_map/dot_general | solution.py:84
  821.4 5.0 gather_fusion.2
  826.4 4.6 select_select_fusion
  831.1 66.2 %reduce-scatter.2.cloned.1.call-done = f32[8,128,128]{2,1,0:T(8,128)} async-done(((f32[64,128,128]{2,1,0:T(8,128)}), f32[8,128,128]{2,1,0:T(8,128)}) %reduce-scatter.2.cloned.1.call-update) | async-done | bytes 524304 | tf_op jit(solution)/shard_map/reduce_scatter | solution.py:100
  (40 shorter events, 0.9 us)
Async XLA Ops:
  6.5 890.7 %reduce-scatter.2.cloned.1.call-start = ((), (), s32[]{:S(2)}) async-start(), calls=%async_computation.2 | async-start | bytes 4718592 | tf_op jit(solution)/shard_map/reduce_scatter | solution.py:100
  43.3 202.3 %collective-permute-start.6 = (f32[32,128,128]{2,1,0:T(8,128)S(1)}, f32[32,128,128]{2,1,0:T(8,128)S(1)}, u32[]{:S(2)}, u32[]{:S(2)}) collective-permute-start(f32[32,128,128]{2,1,0:T(8,128)S(1)} %bitcast.70), channel_id=1, source_target_pairs={{0,384},{32,416},{64,448},{96,480},{128,0},{160,32},{192,64},{224,... | collective-permute-start | bytes 6291464 | tf_op jit(solution)/shard_map/ppermute | solution.py:21
  245.6 1.3 copy-start
  247.0 80.3 %collective-permute-start.7 = (f32[32,128,128]{2,1,0:T(8,128)S(1)}, f32[32,128,128]{2,1,0:T(8,128)}, u32[]{:S(2)}, u32[]{:S(2)}) collective-permute-start(f32[32,128,128]{2,1,0:T(8,128)S(1)} %collective-permute-done.6), channel_id=1, source_target_pairs={{0,384},{32,416},{64,448},{96,480},{128,0},{160,32},{192,64},{224,... | collective-permute-start | bytes 6291464 | tf_op jit(solution)/shard_map/ppermute | solution.py:21
  327.3 178.6 %collective-permute-start.8 = (f32[32,128,128]{2,1,0:T(8,128)}, f32[32,128,128]{2,1,0:T(8,128)}, u32[]{:S(2)}, u32[]{:S(2)}) collective-permute-start(f32[32,128,128]{2,1,0:T(8,128)} %collective-permute-done.7), channel_id=1, source_target_pairs={{0,384},{32,416},{64,448},{96,480},{128,0},{160,32},{192,64},{224,... | collective-permute-start | bytes 6291464 | tf_op jit(solution)/shard_map/ppermute | solution.py:21
  334.1 277.5 %copy-start.2 = (s32[8,2]{0,1:T(2,128)S(1)}, s32[8,2]{0,1:T(2,128)}, u32[]{:S(2)}) copy-start(s32[8,2]{0,1:T(2,128)} %param.4) | copy-start | bytes 196
  334.1 290.9 %copy-start.1 = (s32[64,2]{0,1:T(2,128)S(1)}, s32[64,2]{0,1:T(2,128)}, u32[]{:S(2)}) copy-start(s32[64,2]{0,1:T(2,128)} %param.5) | copy-start | bytes 1540
  509.7 147.3 %collective-permute-start.9 = (f32[32,128,128]{2,1,0:T(8,128)}, f32[32,128,128]{2,1,0:T(8,128)}, u32[]{:S(2)}, u32[]{:S(2)}) collective-permute-start(f32[32,128,128]{2,1,0:T(8,128)} %select_select_fusion.1), channel_id=1, source_target_pairs={{0,480},{32,0},{64,32},{96,64},{128,96},{160,128},{192,160},{224,1... | collective-permute-start | bytes 6291464 | tf_op jit(solution)/shard_map/ppermute | solution.py:21
  617.5 45.3 %collective-permute-start = (s32[32,2]{0,1:T(2,128)S(1)}, s32[32,2]{0,1:T(2,128)S(1)}, u32[]{:S(2)}, u32[]{:S(2)}) collective-permute-start(s32[32,2]{0,1:T(2,128)S(1)} %reshape.231), channel_id=1, source_target_pairs={{0,384},{32,416},{64,448},{96,480},{128,0},{160,32},{192,64},{224,... | collective-permute-start | bytes 776 | tf_op jit(solution)/shard_map/ppermute | solution.py:21
  657.0 72.3 %collective-permute-start.10 = (f32[32,128,128]{2,1,0:T(8,128)}, f32[32,128,128]{2,1,0:T(8,128)}, u32[]{:S(2)}, u32[]{:S(2)}) collective-permute-start(f32[32,128,128]{2,1,0:T(8,128)} %collective-permute-done.9), channel_id=1, source_target_pairs={{0,480},{32,0},{64,32},{96,64},{128,96},{160,128},{192,160},{224,1... | collective-permute-start | bytes 6291464 | tf_op jit(solution)/shard_map/ppermute | solution.py:21
  662.8 44.3 %collective-permute-start.1 = (s32[32,2]{0,1:T(2,128)S(1)}, s32[32,2]{0,1:T(2,128)S(1)}, u32[]{:S(2)}, u32[]{:S(2)}) collective-permute-start(s32[32,2]{0,1:T(2,128)S(1)} %collective-permute-done), channel_id=1, source_target_pairs={{0,384},{32,416},{64,448},{96,480},{128,0},{160,32},{192,64},{224,... | collective-permute-start | bytes 776 | tf_op jit(solution)/shard_map/ppermute | solution.py:21
  707.0 8.3 collective-permute-start.2
  715.4 4.3 collective-permute-start.3
  719.7 4.3 collective-permute-start.4
  724.0 5.3 collective-permute-start.5
  729.3 44.6 %collective-permute-start.11 = (f32[32,128,128]{2,1,0:T(8,128)}, f32[32,128,128]{2,1,0:T(8,128)}, u32[]{:S(2)}, u32[]{:S(2)}) collective-permute-start(f32[32,128,128]{2,1,0:T(8,128)} %collective-permute-done.10), channel_id=1, source_target_pairs={{0,480},{32,0},{64,32},{96,64},{128,96},{160,128},{192,160},{224,1... | collective-permute-start | bytes 6291464 | tf_op jit(solution)/shard_map/ppermute | solution.py:21
Sparse Core Ops, SparseCore 0:
  831.2 65.9 reduce-scatter.1
